TPU v7x, 512 devices: a whole 4x8x8 slice. The times are simulated.
512 devices in a mesh: dp: 2 (over core), ctx: 64 (over z, y), head: 4 (over x).
Axes of the slice: x: 4, y: 8, z: 8, core: 2. Of those that a mesh axis runs over, the one named last changes fastest.
Arguments:
- queries: bfloat16 [2, 8192, 2560], P('dp', 'ctx', 'head'), may hold values from -25 to 25
- keys: bfloat16 [2, 8192, 2560], P('dp', 'ctx', 'head'), may hold values from -25 to 25
- values: bfloat16 [2, 8192, 2560], P('dp', 'ctx', 'head'), may hold values from -6 to 6
- grad_y: bfloat16 [2, 8192, 2560], P('dp', 'ctx', 'head'), may hold values from -6 to 6
- out_gain: float32 [2560], P('head'), may hold values from 0.1 to 1.9
- offsets: int32 [2, 20], P(None, 'head'), may hold values from 0 to 63, as said below
Outputs:
- attended: bfloat16 [2, 8192, 2560], P('dp', 'ctx', 'head')
- query_grad: bfloat16 [2, 8192, 2560], P('dp', 'ctx', 'head')
- key_grad: bfloat16 [2, 8192, 2560], P('dp', 'ctx', 'head')
- value_grad: bfloat16 [2, 8192, 2560], P('dp', 'ctx', 'head')
- gain_grad: float32 [2560], P('head')
Inputs may be any that keep to these rules, and one draw needn't show every extreme that they name: Row 0 holds offsets below 8, row 1 offsets below 64.
All inputs are finite; a program needn't handle non-finite values.
Results may differ from a plain program's by a relative error of at most 0.011.
Values may be sent and summed in bfloat16 or wider, within the bound.
A program may use at most 64 MiB of HBM per device.

v0:
```python
import math
import jax
import jax.numpy as jnp
from jax import lax
from jax.sharding import PartitionSpec as P

HEAD_DIM = 128
SPAN = 4
R1 = 8
EPS = 1e-06


def group_gather(block, axis, group):
    count = lax.axis_size(axis)
    pieces = [block]
    for shift in range(1, group):
        route = []
        for src in range(count):
            base = src - src % group
            route.append((src, base + (src % group + shift) % group))
        pieces.append(lax.ppermute(block, axis, route))
    return jnp.concatenate(pieces, 0)


def pick_rows(source_rows, dilation, shifts):
    row_count, head_count, head_width = source_rows.shape
    grouped = source_rows.reshape(row_count // dilation, dilation, head_count, head_width)
    hit_mask = jnp.arange(dilation, dtype=jnp.int32).reshape(1, dilation, 1, 1) == shifts.reshape(
        1, 1, head_count, 1
    )
    chosen = jnp.where(hit_mask, grouped, jnp.zeros((), source_rows.dtype))
    return jnp.sum(chosen, axis=1, dtype=source_rows.dtype)


def place_rows(row_values, dilation, shifts):
    row_count, head_count, head_width = row_values.shape
    hit_mask = jnp.arange(dilation, dtype=jnp.int32).reshape(1, dilation, 1, 1) == shifts.reshape(
        1, 1, head_count, 1
    )
    spread = jnp.where(hit_mask, row_values[:, None], jnp.zeros((), row_values.dtype))
    return spread.reshape(row_count * dilation, head_count, head_width)


def level_scores(q_rows, k_rows):
    score_scale = 1.0 / math.sqrt(q_rows.shape[-1])
    return (
        jnp.einsum("qhe,khe->hqk", q_rows, k_rows, preferred_element_type=jnp.float32) * score_scale
    )


def attend(q_rows, k_rows, v_rows):
    scores = level_scores(q_rows, k_rows)
    row_max = jnp.max(scores, axis=-1, keepdims=True)
    log_total = row_max[..., 0] + jnp.log(jnp.sum(jnp.exp(scores - row_max), axis=-1))
    soft_rows = jnp.exp(scores - log_total[..., None]).astype(jnp.bfloat16)
    level_out = jnp.einsum("hqk,khe->qhe", soft_rows, v_rows, preferred_element_type=jnp.float32)
    return (level_out, log_total.T)


def score_grads(q_rows, k_rows, v_rows, log_total, grad_low, row_shift):
    score_scale = 1.0 / math.sqrt(q_rows.shape[-1])
    scores = level_scores(q_rows, k_rows)
    exact_soft = jnp.exp(scores - log_total.T[..., None])
    prob_grad = jnp.einsum("qhe,khe->hqk", grad_low, v_rows, preferred_element_type=jnp.float32)
    score_grad = (exact_soft * (prob_grad + row_shift.T[..., None]) * score_scale).astype(
        jnp.bfloat16
    )
    return (score_grad, exact_soft.astype(jnp.bfloat16))


def key_parts(score_grad, soft_low, q_rows, grad_low):
    k_part = jnp.einsum("hqk,qhe->khe", score_grad, q_rows, preferred_element_type=jnp.float32)
    v_part = jnp.einsum("hqk,qhe->khe", soft_low, grad_low, preferred_element_type=jnp.float32)
    return (k_part, v_part)


def query_part(score_grad, k_rows):
    return jnp.einsum("hqk,khe->qhe", score_grad, k_rows, preferred_element_type=jnp.float32)


def split_qkv(packed, head_count):
    width = head_count * HEAD_DIM
    shape = (packed.shape[0], head_count, HEAD_DIM)
    return tuple((packed[:, i * width : (i + 1) * width].reshape(shape) for i in range(3)))


def pack_grads(grad_low, row_shift):
    rows = grad_low.shape[0]
    return jnp.concatenate(
        [grad_low.astype(jnp.float32).reshape(rows, -1), row_shift.astype(jnp.float32)], 1
    )


def unpack_grads(packed, head_count):
    width = head_count * HEAD_DIM
    grad_low = packed[:, :width].astype(jnp.bfloat16).reshape(-1, head_count, HEAD_DIM)
    return (grad_low, packed[:, width:])


def shards(queries, keys, values, grad_y, out_gain, offsets):
    tokens = queries.shape[1]
    flat_width = queries.shape[2]
    head_count = flat_width // HEAD_DIM
    row_shape = (tokens, head_count, HEAD_DIM)
    q_own = queries[0].reshape(row_shape)
    k_own = keys[0].reshape(row_shape)
    v_own = values[0].reshape(row_shape)
    ctx_size = lax.axis_size("ctx")
    my_place = lax.axis_index("ctx")
    mid_shift = offsets[0]
    top_shift = offsets[1]
    positions = jnp.arange(tokens, dtype=jnp.int32)
    mid_hit = (positions % R1)[:, None] == mid_shift[None, :]
    top_hit = (positions % ctx_size)[:, None] == top_shift[None, :]
    mid_pack = jnp.concatenate(
        [pick_rows(x, R1, mid_shift).reshape(-1, flat_width) for x in (q_own, k_own, v_own)], 1
    )
    top_pack = jnp.concatenate(
        [pick_rows(x, ctx_size, top_shift).reshape(-1, flat_width) for x in (q_own, k_own, v_own)],
        1,
    )
    mid_rows = mid_pack.shape[0]
    top_rows = top_pack.shape[0]
    mid_all = group_gather(mid_pack, "ctx", SPAN)
    top_all = lax.all_gather(top_pack, "ctx", axis=0, tiled=True)
    mid_q, mid_k, mid_v = split_qkv(mid_all, head_count)
    top_q, top_k, top_v = split_qkv(top_all, head_count)
    top_start = my_place * top_rows
    base_out, base_total = attend(q_own, k_own, v_own)
    mid_out_all, mid_total_all = attend(mid_q, mid_k, mid_v)
    top_out_all, top_total_all = attend(top_q, top_k, top_v)
    mid_out = mid_out_all[:mid_rows]
    mid_total = mid_total_all[:mid_rows]
    top_out = lax.dynamic_slice_in_dim(top_out_all, top_start, top_rows, 0)
    top_total = lax.dynamic_slice_in_dim(top_total_all, top_start, top_rows, 0)
    mid_full = place_rows(mid_total[..., None], R1, mid_shift)[..., 0]
    top_full = place_rows(top_total[..., None], ctx_size, top_shift)[..., 0]
    row_max = jnp.maximum(base_total, jnp.where(mid_hit, mid_full, base_total))
    row_max = jnp.maximum(row_max, jnp.where(top_hit, top_full, base_total))
    base_expo = jnp.exp(base_total - row_max)
    mid_expo = jnp.where(mid_hit, jnp.exp(mid_full - row_max), 0.0)
    top_expo = jnp.where(top_hit, jnp.exp(top_full - row_max), 0.0)
    denom = base_expo + mid_expo + top_expo
    base_share = base_expo / denom
    mid_share = mid_expo / denom
    top_share = top_expo / denom
    attn = (
        base_share[..., None] * base_out
        + mid_share[..., None] * place_rows(mid_out, R1, mid_shift)
        + top_share[..., None] * place_rows(top_out, ctx_size, top_shift)
    )
    inv_rms = lax.rsqrt(jnp.mean(attn * attn, axis=-1, keepdims=True) + EPS)
    normed = attn * inv_rms
    gain_rows = out_gain.reshape(head_count, HEAD_DIM)
    attended = (normed * gain_rows).astype(jnp.bfloat16).reshape(1, tokens, flat_width)
    grad_full = grad_y[0].reshape(row_shape).astype(jnp.float32)
    gain_part = jnp.sum(grad_full * normed, axis=0).reshape(flat_width)
    grad_norm = grad_full * gain_rows
    grad_attn = inv_rms * (
        grad_norm - normed * jnp.mean(grad_norm * normed, axis=-1, keepdims=True)
    )
    inner = jnp.sum(grad_attn * attn, axis=-1)
    base_low = (base_share[..., None] * grad_attn).astype(jnp.bfloat16)
    base_shift = -(base_share * inner)
    base_grad, base_soft = score_grads(q_own, k_own, v_own, base_total, base_low, base_shift)
    base_dq = query_part(base_grad, k_own)
    base_dk, base_dv = key_parts(base_grad, base_soft, q_own, base_low)
    mid_sel = pick_rows(mid_share[..., None], R1, mid_shift)[..., 0]
    mid_low = (mid_sel[..., None] * pick_rows(grad_attn, R1, mid_shift)).astype(jnp.bfloat16)
    mid_row_shift = -(mid_sel * pick_rows(inner[..., None], R1, mid_shift)[..., 0])
    top_sel = pick_rows(top_share[..., None], ctx_size, top_shift)[..., 0]
    top_low = (top_sel[..., None] * pick_rows(grad_attn, ctx_size, top_shift)).astype(jnp.bfloat16)
    top_row_shift = -(top_sel * pick_rows(inner[..., None], ctx_size, top_shift)[..., 0])
    mid_low_all, mid_shift_all = unpack_grads(
        group_gather(pack_grads(mid_low, mid_row_shift), "ctx", SPAN), head_count
    )
    top_grads = pack_grads(top_low, top_row_shift)
    gain_row = jnp.pad(gain_part, (0, top_grads.shape[1] - flat_width))[None]
    gathered = lax.all_gather(jnp.concatenate([top_grads, gain_row], 0), "ctx", axis=0)
    top_low_all, top_shift_all = unpack_grads(
        gathered[:, :top_rows].reshape(-1, top_grads.shape[1]), head_count
    )
    gain_grad = lax.psum(jnp.sum(gathered[:, top_rows, :flat_width], axis=0), "dp")
    mid_grad, mid_soft = score_grads(mid_q, mid_k, mid_v, mid_total_all, mid_low_all, mid_shift_all)
    mid_dq = query_part(mid_grad[:, :mid_rows], mid_k)
    mid_dk, mid_dv = key_parts(
        mid_grad[:, :, :mid_rows], mid_soft[:, :, :mid_rows], mid_q, mid_low_all
    )
    top_grad, top_soft = score_grads(top_q, top_k, top_v, top_total_all, top_low_all, top_shift_all)
    own_grad = lax.dynamic_slice_in_dim(top_grad, top_start, top_rows, 1)
    top_dq = query_part(own_grad, top_k)
    key_grad_cols = lax.dynamic_slice_in_dim(top_grad, top_start, top_rows, 2)
    key_soft_cols = lax.dynamic_slice_in_dim(top_soft, top_start, top_rows, 2)
    top_dk, top_dv = key_parts(key_grad_cols, key_soft_cols, top_q, top_low_all)
    query_grad = (
        base_dq + place_rows(mid_dq, R1, mid_shift) + place_rows(top_dq, ctx_size, top_shift)
    )
    key_grad = base_dk + place_rows(mid_dk, R1, mid_shift) + place_rows(top_dk, ctx_size, top_shift)
    value_grad = (
        base_dv + place_rows(mid_dv, R1, mid_shift) + place_rows(top_dv, ctx_size, top_shift)
    )
    out_shape = (1, tokens, flat_width)
    return (
        attended,
        query_grad.astype(jnp.bfloat16).reshape(out_shape),
        key_grad.astype(jnp.bfloat16).reshape(out_shape),
        value_grad.astype(jnp.bfloat16).reshape(out_shape),
        gain_grad,
    )


def solution(mesh):
    in_specs = (
        P("dp", "ctx", "head"),
        P("dp", "ctx", "head"),
        P("dp", "ctx", "head"),
        P("dp", "ctx", "head"),
        P("head"),
        P(None, "head"),
    )
    out_specs = (
        P("dp", "ctx", "head"),
        P("dp", "ctx", "head"),
        P("dp", "ctx", "head"),
        P("dp", "ctx", "head"),
        P("head"),
    )
    return jax.shard_map(shards, mesh=mesh, in_specs=in_specs, out_specs=out_specs, check_vma=False)
```

profile of v0, /device:TPU:1, one launch (start us, length us, event | category | flops | bytes accessed | tf_op | source)
XLA Modules:
  0.0 159.5 jit_solution(9887099655481750333)
XLA Ops:
  0.6 0.8 slice_bitcast_fusion.5
  1.5 1.5 fusion.24
  3.0 6.1 %collective-permute-start.2 = (bf16[16,1920]{1,0:T(8,128)(2,1)S(1)}, bf16[16,1920]{1,0:T(8,128)(2,1)S(1)}, u32[]{:S(2)}, u32[]{:S(2)}) collective-permute-start(bf16[16,1920]{1,0:T(8,128)(2,1)S(1)} %bitcast_dynamic-update-slice_fusion), channel_id=1, source_target_pairs={{0,12},{4,0},{8,4},{12,8},{16,28},{20,16},{24,20},{28,24},{32,44},... | collective-permute-start | bytes 184328 | tf_op jit(solution)/shard_map/ppermute | solution.py:21
  9.1 1.9 %collective-permute-start.1 = (bf16[16,1920]{1,0:T(8,128)(2,1)S(1)}, bf16[16,1920]{1,0:T(8,128)(2,1)S(1)}, u32[]{:S(2)}, u32[]{:S(2)}) collective-permute-start(bf16[16,1920]{1,0:T(8,128)(2,1)S(1)} %bitcast_dynamic-update-slice_fusion), channel_id=1, source_target_pairs={{0,8},{4,12},{8,0},{12,4},{16,24},{20,28},{24,16},{28,20},{32,40},... | collective-permute-start | bytes 184328 | tf_op jit(solution)/shard_map/ppermute | solution.py:21
  11.0 2.3 %collective-permute-start = (bf16[16,1920]{1,0:T(8,128)(2,1)S(1)}, bf16[16,1920]{1,0:T(8,128)(2,1)S(1)}, u32[]{:S(2)}, u32[]{:S(2)}) collective-permute-start(bf16[16,1920]{1,0:T(8,128)(2,1)S(1)} %bitcast_dynamic-update-slice_fusion), channel_id=1, source_target_pairs={{0,4},{4,8},{8,12},{12,0},{16,20},{20,24},{24,28},{28,16},{32,36},... | collective-permute-start | bytes 184328 | tf_op jit(solution)/shard_map/ppermute | solution.py:21
  13.4 0.2 copy.294
  13.6 0.7 copy-done.1
  14.5 0.7 copy-done.2
  15.4 0.2 reshape_reshape_squeeze.21
  15.6 0.2 reshape_reshape_squeeze.22
  15.8 0.2 reshape_reshape_squeeze.23
  16.4 0.3 copy-done.8
  17.0 0.3 select_reduce_fusion.2
  17.4 44.2 %all-gather.1 = bf16[64,2,1920]{2,1,0:T(2,128)(2,1)S(1)} all-gather(bf16[1,2,1920]{2,1,0:T(2,128)(2,1)S(1)} %maximum_bitcast_fusion.2), channel_id=1, replica_groups=mesh['dp'=2,'ctx'=64,'head'=4] {'ctx'}, dimensions={0}, use_global_device_ids=true | all-gather | bytes 499200 | tf_op jit(solution)/shard_map/all_gather | solution.py:125
  61.5 0.2 reshape.375
  61.8 0.2 copy.308
  62.0 0.2 copy.316
  62.1 0.2 copy.307
  62.3 0.3 fusion.67
  63.0 0.3 fusion.70
  63.4 0.3 fusion.69
  63.8 0.2 fusion.68
  64.5 0.2 convolution_bitcast_fusion.4
  65.0 0.2 fusion.20
  65.3 0.5 multiply_reduce_fusion.3
  65.8 0.7 copy-done.9
  66.5 0.8 multiply_reduce_fusion.2
  67.3 0.3 fusion.19
  67.6 0.2 multiply_reduce_fusion.1
  68.2 0.6 pad_maximum_fusion.2
  68.9 3.9 %collective-permute-start.5 = (f32[16,645]{1,0:T(8,128)}, f32[16,645]{1,0:T(8,128)}, u32[]{:S(2)}, u32[]{:S(2)}) collective-permute-start(f32[16,645]{1,0:T(8,128)} %pad_maximum_fusion.2), channel_id=1, source_target_pairs={{0,12},{4,0},{8,4},{12,8},{16,28},{20,16},{24,20},{28,24},{32,44},... | collective-permute-start | bytes 123848 | tf_op jit(solution)/shard_map/ppermute | solution.py:21
  72.8 2.8 %collective-permute-start.4 = (f32[16,645]{1,0:T(8,128)}, f32[16,645]{1,0:T(8,128)}, u32[]{:S(2)}, u32[]{:S(2)}) collective-permute-start(f32[16,645]{1,0:T(8,128)} %pad_maximum_fusion.2), channel_id=1, source_target_pairs={{0,8},{4,12},{8,0},{12,4},{16,24},{20,28},{24,16},{28,20},{32,40},... | collective-permute-start | bytes 123848 | tf_op jit(solution)/shard_map/ppermute | solution.py:21
  75.6 1.9 %collective-permute-start.3 = (f32[16,645]{1,0:T(8,128)}, f32[16,645]{1,0:T(8,128)}, u32[]{:S(2)}, u32[]{:S(2)}) collective-permute-start(f32[16,645]{1,0:T(8,128)} %pad_maximum_fusion.2), channel_id=1, source_target_pairs={{0,4},{4,8},{8,12},{12,0},{16,20},{20,24},{24,28},{28,16},{32,36},... | collective-permute-start | bytes 123848 | tf_op jit(solution)/shard_map/ppermute | solution.py:21
  77.5 0.2 fusion.18
  78.2 38.9 %all-gather.2 = f32[64,3,645]{2,1,0:T(4,128)S(1)} all-gather(f32[1,3,645]{2,1,0:T(4,128)S(1)} %maximum_bitcast_fusion.1), channel_id=2, replica_groups=mesh['dp'=2,'ctx'=64,'head'=4] {'ctx'}, dimensions={0}, use_global_device_ids=true | all-gather | bytes 503100 | tf_op jit(solution)/shard_map/all_gather | solution.py:179
  117.2 1.0 reshape.365
  118.2 0.8 slice_bitcast_fusion.3
  119.1 1.0 slice.110
  120.1 0.2 copy.338
  120.3 0.9 convolution_bitcast_fusion.9
  121.2 0.3 fusion.16
  121.5 0.2 convolution_bitcast_fusion.10
  121.7 0.4 convolution_bitcast_fusion.8
  122.1 0.4 fusion.17
  122.5 0.2 slice_reduce_fusion
  122.7 0.7 copy-done.4
  123.4 0.2 copy.319
  123.5 0.8 copy.357
  124.4 0.2 bitcast_select_fusion
  124.5 28.0 %psum.7 = f32[640]{0:T(1024)} all-reduce(f32[640]{0:T(1024)S(1)} %slice_reduce_fusion), channel_id=1, replica_groups=mesh['dp'=2,'ctx'=64,'head'=4] {'dp'}, use_global_device_ids=true, to_apply=%region_23.24 | all-reduce | flops 640 | bytes 5120 | tf_op jit(solution)/shard_map/psum | solution.py:183
  152.5 0.9 pad_maximum_fusion.1
  153.4 0.9 convolution_bitcast_fusion.5
  154.2 0.8 maximum_bitcast_fusion
  155.2 0.2 multiply_convert_fusion.2
  155.5 0.2 convolution_bitcast_fusion.7
  155.7 0.3 fusion.14
  156.0 0.2 copy.350
  156.1 0.8 copy.359
  157.0 0.3 fusion.13
  157.2 0.2 copy.345
  157.4 0.8 copy.358
  158.2 0.3 fusion.15
  158.5 0.2 copy.356
  158.7 0.8 copy.360
  (82 shorter events, 3.9 us)
Async XLA Ops:
  1.5 11.9 %copy-start = (bf16[1,128,640]{2,1,0:T(8,128)(2,1)S(1)}, bf16[1,128,640]{2,1,0:T(8,128)(2,1)}, u32[]{:S(2)}) copy-start(bf16[1,128,640]{2,1,0:T(8,128)(2,1)} %param.6) | copy-start | bytes 491524
  3.0 60.7 %collective-permute-start.2 = (bf16[16,1920]{1,0:T(8,128)(2,1)S(1)}, bf16[16,1920]{1,0:T(8,128)(2,1)S(1)}, u32[]{:S(2)}, u32[]{:S(2)}) collective-permute-start(bf16[16,1920]{1,0:T(8,128)(2,1)S(1)} %bitcast_dynamic-update-slice_fusion), channel_id=1, source_target_pairs={{0,12},{4,0},{8,4},{12,8},{16,28},{20,16},{24,20},{28,24},{32,44},... | collective-permute-start | bytes 184328 | tf_op jit(solution)/shard_map/ppermute | solution.py:21
  9.1 54.7 %collective-permute-start.1 = (bf16[16,1920]{1,0:T(8,128)(2,1)S(1)}, bf16[16,1920]{1,0:T(8,128)(2,1)S(1)}, u32[]{:S(2)}, u32[]{:S(2)}) collective-permute-start(bf16[16,1920]{1,0:T(8,128)(2,1)S(1)} %bitcast_dynamic-update-slice_fusion), channel_id=1, source_target_pairs={{0,8},{4,12},{8,0},{12,4},{16,24},{20,28},{24,16},{28,20},{32,40},... | collective-permute-start | bytes 184328 | tf_op jit(solution)/shard_map/ppermute | solution.py:21
  11.0 52.7 %collective-permute-start = (bf16[16,1920]{1,0:T(8,128)(2,1)S(1)}, bf16[16,1920]{1,0:T(8,128)(2,1)S(1)}, u32[]{:S(2)}, u32[]{:S(2)}) collective-permute-start(bf16[16,1920]{1,0:T(8,128)(2,1)S(1)} %bitcast_dynamic-update-slice_fusion), channel_id=1, source_target_pairs={{0,4},{4,8},{8,12},{12,0},{16,20},{20,24},{24,28},{28,16},{32,36},... | collective-permute-start | bytes 184328 | tf_op jit(solution)/shard_map/ppermute | solution.py:21
  13.4 0.9 copy-start.1
  14.3 0.9 copy-start.2
  15.8 0.9 copy-start.8
  62.7 0.7 copy-start.3
  63.8 0.6 copy-start.6
  64.1 0.6 copy-start.5
  65.8 0.7 copy-start.9
  68.9 83.7 %collective-permute-start.5 = (f32[16,645]{1,0:T(8,128)}, f32[16,645]{1,0:T(8,128)}, u32[]{:S(2)}, u32[]{:S(2)}) collective-permute-start(f32[16,645]{1,0:T(8,128)} %pad_maximum_fusion.2), channel_id=1, source_target_pairs={{0,12},{4,0},{8,4},{12,8},{16,28},{20,16},{24,20},{28,24},{32,44},... | collective-permute-start | bytes 123848 | tf_op jit(solution)/shard_map/ppermute | solution.py:21
  72.8 79.7 %collective-permute-start.4 = (f32[16,645]{1,0:T(8,128)}, f32[16,645]{1,0:T(8,128)}, u32[]{:S(2)}, u32[]{:S(2)}) collective-permute-start(f32[16,645]{1,0:T(8,128)} %pad_maximum_fusion.2), channel_id=1, source_target_pairs={{0,8},{4,12},{8,0},{12,4},{16,24},{20,28},{24,16},{28,20},{32,40},... | collective-permute-start | bytes 123848 | tf_op jit(solution)/shard_map/ppermute | solution.py:21
  75.6 76.9 %collective-permute-start.3 = (f32[16,645]{1,0:T(8,128)}, f32[16,645]{1,0:T(8,128)}, u32[]{:S(2)}, u32[]{:S(2)}) collective-permute-start(f32[16,645]{1,0:T(8,128)} %pad_maximum_fusion.2), channel_id=1, source_target_pairs={{0,4},{4,8},{8,12},{12,0},{16,20},{20,24},{24,28},{28,16},{32,36},... | collective-permute-start | bytes 123848 | tf_op jit(solution)/shard_map/ppermute | solution.py:21
  122.4 0.9 copy-start.4
  154.2 1.0 copy-start.7
where the time goes:
time: 160 us
  blocking collectives  111 us (69%)
  starting transfers between devices  19 us (12%)
  local copies, waits for them, and re-layouts  15.2 us (10%)
  other arithmetic  7.09 us (4%)
  matrix products  6.04 us (4%)
    all_gather x1, blocking collectives, shards(): top_all = lax.all_gather(top_pack, 'ctx', axis=0, tiled=True)  44.2 us
    all_gather x1, blocking collectives, shards(): lax.all_gather(jnp.concatenate([top_grads, gain_row], 0), 'ctx', axis=0)  38.9 us
    psum x1, blocking collectives, shards(): lax.psum(jnp.sum(gathered[:, top_rows, :flat_width], axis=0), 'dp')  28 us
    ppermute x6, starting transfers between devices, group_gather(): pieces.append(lax.ppermute(block, axis, route))  19 us
    unnamed x34, local copies, waits for them, and re-layouts  7.85 us
  transfers between devices with their start and end apart: 6, of which 0 were waited for; matrix products, arithmetic and copies ran while one was open for 7% of the time, Pallas kernels for 0%

commit v1 on v0

--- a/solution.py
+++ b/solution.py
@@ -122,7 +122,9 @@
     mid_rows = mid_pack.shape[0]
     top_rows = top_pack.shape[0]
     mid_all = group_gather(mid_pack, "ctx", SPAN)
-    top_all = lax.all_gather(top_pack, "ctx", axis=0, tiled=True)
+    top_all = lax.all_to_all(
+        jnp.concatenate([top_pack] * lax.axis_size("ctx"), axis=0), "ctx", 0, 0, tiled=True
+    )
     mid_q, mid_k, mid_v = split_qkv(mid_all, head_count)
     top_q, top_k, top_v = split_qkv(top_all, head_count)
     top_start = my_place * top_rows

time: 160 us -> 136 us (0.85)
  blocking collectives: 111 us -> 55.8 us
  starting transfers between devices: 19 us -> 34.9 us
  waiting for transfers between devices: 0.02 us -> 11.6 us
  local copies, waits for them, and re-layouts: 15.2 us -> 18.3 us
    all_gather x1 -> x0, blocking collectives: 44.2 us -> none  [shards(): top_all = lax.all_gather(top_pack, 'ctx', axis=0, tiled=True)]
    all_to_all x0 -> x1, starting transfers between devices: none -> 14.6 us  [shards(): lax.all_to_all(jnp.concatenate([top_pack] * lax.axis_size('ctx'), axis=0)...]
    all_to_all x0 -> x1, waiting for transfers between devices: none -> 11.6 us  [shards(): lax.all_to_all(jnp.concatenate([top_pack] * lax.axis_size('ctx'), axis=0)...]
    psum x1, blocking collectives: 28 us -> 18.7 us  [shards(): lax.psum(jnp.sum(gathered[:, top_rows, :flat_width], axis=0), 'dp')]
    all_gather x1, blocking collectives: 38.9 us -> 37.1 us  [shards(): lax.all_gather(jnp.concatenate([top_grads, gain_row], 0), 'ctx', axis=0)]
    unnamed x34 -> x49, local copies, waits for them, and re-layouts: 7.85 us -> 8.77 us
  transfers between devices with their start and end apart: 6 -> 7, of which waited for: 0 -> 1; matrix products, arithmetic and copies ran while one was open for 7% -> 9% of each run, Pallas kernels for 0% -> 0%
where the time goes in v1:
time: 136 us
  blocking collectives  55.8 us (41%)
  starting transfers between devices  34.9 us (26%)
  local copies, waits for them, and re-layouts  18.3 us (13%)
  waiting for transfers between devices  11.6 us (9%)
  other arithmetic  7.6 us (6%)
  matrix products  6.05 us (4%)
    all_gather x1, blocking collectives, shards(): lax.all_gather(jnp.concatenate([top_grads, gain_row], 0), 'ctx', axis=0)  37.1 us
    ppermute x6, starting transfers between devices, group_gather(): pieces.append(lax.ppermute(block, axis, route))  20.3 us
    psum x1, blocking collectives, shards(): lax.psum(jnp.sum(gathered[:, top_rows, :flat_width], axis=0), 'dp')  18.7 us
    all_to_all x1, starting transfers between devices, shards(): lax.all_to_all(jnp.concatenate([top_pack] * lax.axis_size('ctx'), axis=0)...  14.6 us
    all_to_all x1, waiting for transfers between devices, shards(): lax.all_to_all(jnp.concatenate([top_pack] * lax.axis_size('ctx'), axis=0)...  11.6 us
    unnamed x49, local copies, waits for them, and re-layouts  8.77 us
  transfers between devices with their start and end apart: 7, of which 1 were waited for; matrix products, arithmetic and copies ran while one was open for 9% of the time, Pallas kernels for 0%

profile of v1, /device:TPU:1, one launch (start us, length us, event | category | flops | bytes accessed | tf_op | source)
XLA Modules:
  0.0 135.5 jit_solution(14557936050875243890)
XLA Ops:
  0.6 0.8 slice_bitcast_fusion.5
  1.4 0.5 copy-done.12
  2.0 1.5 %fusion.24 = (bf16[16,5,128]{2,0,1:T(8,128)(2,1)S(1)}, bf16[16,5,128]{2,0,1:T(8,128)(2,1)S(1)}, bf16[16,5,128]{2,0,1:T(8,128)(2,1)S(1)}) fusion(pred[8,5]{0,1:T(8,128)(4,1)S(1)} %iota_compare_fusion.1, bf16[1,128,640]{2,1,0:T(8,128)(2,1)} %param.6, bf16[1,128,640]{2,1,0:T(8,128)(2,1)} %param.7, bf16[1,128,640]{2,1,0:T(8,128)(2,1)} %param.8), kind=kLoop, calls=%fused_computation.70 | loop fusion | flops 460800 | bytes 553000 | tf_op jit(solution)/shard_map/reduce_sum | solution.py:32
  3.6 6.2 %collective-permute-start.2 = (bf16[16,1920]{1,0:T(8,128)(2,1)S(1)}, bf16[16,1920]{1,0:T(8,128)(2,1)S(1)}, u32[]{:S(2)}, u32[]{:S(2)}) collective-permute-start(bf16[16,1920]{1,0:T(8,128)(2,1)S(1)} %bitcast_dynamic-update-slice_fusion), channel_id=1, source_target_pairs={{0,12},{4,0},{8,4},{12,8},{16,28},{20,16},{24,20},{28,24},{32,44},... | collective-permute-start | bytes 184328 | tf_op jit(solution)/shard_map/ppermute | solution.py:21
  9.8 1.9 %collective-permute-start.1 = (bf16[16,1920]{1,0:T(8,128)(2,1)S(1)}, bf16[16,1920]{1,0:T(8,128)(2,1)S(1)}, u32[]{:S(2)}, u32[]{:S(2)}) collective-permute-start(bf16[16,1920]{1,0:T(8,128)(2,1)S(1)} %bitcast_dynamic-update-slice_fusion), channel_id=1, source_target_pairs={{0,8},{4,12},{8,0},{12,4},{16,24},{20,28},{24,16},{28,20},{32,40},... | collective-permute-start | bytes 184328 | tf_op jit(solution)/shard_map/ppermute | solution.py:21
  11.7 2.3 %collective-permute-start = (bf16[16,1920]{1,0:T(8,128)(2,1)S(1)}, bf16[16,1920]{1,0:T(8,128)(2,1)S(1)}, u32[]{:S(2)}, u32[]{:S(2)}) collective-permute-start(bf16[16,1920]{1,0:T(8,128)(2,1)S(1)} %bitcast_dynamic-update-slice_fusion), channel_id=1, source_target_pairs={{0,4},{4,8},{8,12},{12,0},{16,20},{20,24},{24,28},{28,16},{32,36},... | collective-permute-start | bytes 184328 | tf_op jit(solution)/shard_map/ppermute | solution.py:21
  14.1 0.2 reshape_reshape_squeeze.21
  14.3 0.2 reshape_reshape_squeeze.22
  14.5 0.7 copy-done.2
  15.2 0.2 reshape_reshape_squeeze.23
  15.6 0.3 select_reduce_fusion.2
  15.9 1.0 concatenate.27
  17.0 1.0 all_to_all.8
  17.9 14.6 %all-to-all-start = ((bf16[64,2,1920]{2,1,0:T(2,128)(2,1)}), bf16[64,2,1920]{2,1,0:T(2,128)(2,1)S(1)}, u32[]{:S(2)}, u32[]{:S(2)}) async-start(bf16[64,2,1920]{2,1,0:T(2,128)(2,1)} %all_to_all.8), calls=%async_computation | async-start | bytes 983040 | tf_op jit(solution)/shard_map/all_to_all | solution.py:125
  32.7 0.2 copy.227
  33.3 0.5 copy-done.8
  34.1 0.3 fusion.69
  34.5 0.5 and_select_fusion
  35.1 0.2 fusion.68
  35.7 0.2 convolution_bitcast_fusion.4
  35.9 0.2 copy-done.5
  36.2 11.6 %all-to-all-done = bf16[64,2,1920]{2,1,0:T(2,128)(2,1)S(1)} async-done(((bf16[64,2,1920]{2,1,0:T(2,128)(2,1)}), bf16[64,2,1920]{2,1,0:T(2,128)(2,1)S(1)}, u32[]{:S(2)}, u32[]{:S(2)}) %all-to-all-start) | async-done | bytes 491552 | tf_op jit(solution)/shard_map/all_to_all | solution.py:125
  47.8 0.2 all_to_all.10
  48.2 0.2 copy.248
  48.6 0.3 fusion.67
  49.2 0.3 copy-done.17
  49.5 0.4 copy-done.13
  50.2 0.3 fusion.70
  50.5 0.2 fusion.20
  50.7 0.5 multiply_reduce_fusion.3
  51.3 0.7 copy-done.9
  51.9 0.8 multiply_reduce_fusion.2
  52.8 0.3 fusion.19
  53.7 0.6 pad_maximum_fusion.2
  54.3 5.3 %collective-permute-start.5 = (f32[16,645]{1,0:T(8,128)}, f32[16,645]{1,0:T(8,128)}, u32[]{:S(2)}, u32[]{:S(2)}) collective-permute-start(f32[16,645]{1,0:T(8,128)} %pad_maximum_fusion.2), channel_id=1, source_target_pairs={{0,12},{4,0},{8,4},{12,8},{16,28},{20,16},{24,20},{28,24},{32,44},... | collective-permute-start | bytes 123848 | tf_op jit(solution)/shard_map/ppermute | solution.py:21
  59.6 1.9 %collective-permute-start.4 = (f32[16,645]{1,0:T(8,128)}, f32[16,645]{1,0:T(8,128)}, u32[]{:S(2)}, u32[]{:S(2)}) collective-permute-start(f32[16,645]{1,0:T(8,128)} %pad_maximum_fusion.2), channel_id=1, source_target_pairs={{0,8},{4,12},{8,0},{12,4},{16,24},{20,28},{24,16},{28,20},{32,40},... | collective-permute-start | bytes 123848 | tf_op jit(solution)/shard_map/ppermute | solution.py:21
  61.5 2.6 %collective-permute-start.3 = (f32[16,645]{1,0:T(8,128)}, f32[16,645]{1,0:T(8,128)}, u32[]{:S(2)}, u32[]{:S(2)}) collective-permute-start(f32[16,645]{1,0:T(8,128)} %pad_maximum_fusion.2), channel_id=1, source_target_pairs={{0,4},{4,8},{8,12},{12,0},{16,20},{20,24},{24,28},{28,16},{32,36},... | collective-permute-start | bytes 123848 | tf_op jit(solution)/shard_map/ppermute | solution.py:21
  64.1 0.2 fusion.18
  64.4 0.4 copy-done.11
  65.2 37.1 %all-gather.1 = f32[64,3,645]{2,1,0:T(4,128)S(1)} all-gather(f32[1,3,645]{2,1,0:T(4,128)S(1)} %maximum_bitcast_fusion.1), channel_id=2, replica_groups=mesh['dp'=2,'ctx'=64,'head'=4] {'ctx'}, dimensions={0}, use_global_device_ids=true | all-gather | bytes 503100 | tf_op jit(solution)/shard_map/all_gather | solution.py:181
  102.4 1.0 reshape.367
  103.4 0.8 slice_bitcast_fusion.3
  104.3 1.0 slice.110
  105.3 0.2 copy.270
  105.5 0.9 convolution_bitcast_fusion.9
  106.4 0.3 fusion.16
  106.7 0.2 convolution_bitcast_fusion.10
  106.9 0.4 convolution_bitcast_fusion.8
  107.3 0.4 fusion.17
  107.7 0.2 slice_reduce_fusion
  107.9 0.7 copy-done.4
  108.8 0.8 copy.289
  109.8 18.7 %psum.7 = f32[640]{0:T(1024)} all-reduce(f32[640]{0:T(1024)S(1)} %slice_reduce_fusion), channel_id=1, replica_groups=mesh['dp'=2,'ctx'=64,'head'=4] {'dp'}, use_global_device_ids=true, to_apply=%region_23.24 | all-reduce | flops 640 | bytes 5120 | tf_op jit(solution)/shard_map/psum | solution.py:185
  128.5 0.9 pad_maximum_fusion.1
  129.4 0.9 convolution_bitcast_fusion.5
  130.2 0.8 maximum_bitcast_fusion
  131.2 0.2 multiply_convert_fusion.2
  131.5 0.2 convolution_bitcast_fusion.7
  131.7 0.3 fusion.14
  132.1 0.8 copy.291
  133.0 0.3 fusion.13
  133.4 0.8 copy.290
  134.2 0.3 fusion.15
  134.7 0.8 copy.292
  (101 shorter events, 5.1 us)
Async XLA Ops:
  1.4 0.5 copy-start.12
  1.4 14.0 %copy-start.14 = (s32[5]{0:T(128)}, s32[5]{0:T(128)S(1)}, u32[]{:S(2)}) copy-start(s32[5]{0:T(128)S(1)} %get-tuple-element.57) | copy-start | bytes 64
  2.0 12.1 %copy-start = (bf16[1,128,640]{2,1,0:T(8,128)(2,1)S(1)}, bf16[1,128,640]{2,1,0:T(8,128)(2,1)}, u32[]{:S(2)}) copy-start(bf16[1,128,640]{2,1,0:T(8,128)(2,1)} %param.6) | copy-start | bytes 491524
  3.6 10.7 %copy-start.1 = (bf16[1,128,640]{2,1,0:T(8,128)(2,1)S(1)}, bf16[1,128,640]{2,1,0:T(8,128)(2,1)}, u32[]{:S(2)}) copy-start(bf16[1,128,640]{2,1,0:T(8,128)(2,1)} %param.7) | copy-start | bytes 491524
  3.6 31.4 %collective-permute-start.2 = (bf16[16,1920]{1,0:T(8,128)(2,1)S(1)}, bf16[16,1920]{1,0:T(8,128)(2,1)S(1)}, u32[]{:S(2)}, u32[]{:S(2)}) collective-permute-start(bf16[16,1920]{1,0:T(8,128)(2,1)S(1)} %bitcast_dynamic-update-slice_fusion), channel_id=1, source_target_pairs={{0,12},{4,0},{8,4},{12,8},{16,28},{20,16},{24,20},{28,24},{32,44},... | collective-permute-start | bytes 184328 | tf_op jit(solution)/shard_map/ppermute | solution.py:21
  9.8 25.2 %collective-permute-start.1 = (bf16[16,1920]{1,0:T(8,128)(2,1)S(1)}, bf16[16,1920]{1,0:T(8,128)(2,1)S(1)}, u32[]{:S(2)}, u32[]{:S(2)}) collective-permute-start(bf16[16,1920]{1,0:T(8,128)(2,1)S(1)} %bitcast_dynamic-update-slice_fusion), channel_id=1, source_target_pairs={{0,8},{4,12},{8,0},{12,4},{16,24},{20,28},{24,16},{28,20},{32,40},... | collective-permute-start | bytes 184328 | tf_op jit(solution)/shard_map/ppermute | solution.py:21
  11.7 23.3 %collective-permute-start = (bf16[16,1920]{1,0:T(8,128)(2,1)S(1)}, bf16[16,1920]{1,0:T(8,128)(2,1)S(1)}, u32[]{:S(2)}, u32[]{:S(2)}) collective-permute-start(bf16[16,1920]{1,0:T(8,128)(2,1)S(1)} %bitcast_dynamic-update-slice_fusion), channel_id=1, source_target_pairs={{0,4},{4,8},{8,12},{12,0},{16,20},{20,24},{24,28},{28,16},{32,36},... | collective-permute-start | bytes 184328 | tf_op jit(solution)/shard_map/ppermute | solution.py:21
  14.3 0.9 copy-start.2
  15.5 17.6 %copy-start.10 = (pred[64,5]{0,1:T(8,128)(4,1)}, pred[64,5]{0,1:T(8,128)(4,1)S(1)}, u32[]{:S(2)}) copy-start(pred[64,5]{0,1:T(8,128)(4,1)S(1)} %iota_compare_fusion) | copy-start | bytes 964
  17.9 29.9 %all-to-all-start = ((bf16[64,2,1920]{2,1,0:T(2,128)(2,1)}), bf16[64,2,1920]{2,1,0:T(2,128)(2,1)S(1)}, u32[]{:S(2)}, u32[]{:S(2)}) async-start(bf16[64,2,1920]{2,1,0:T(2,128)(2,1)} %all_to_all.8), calls=%async_computation | async-start | bytes 983040 | tf_op jit(solution)/shard_map/all_to_all | solution.py:125
  32.9 0.9 copy-start.8
  35.1 0.6 copy-start.6
  35.5 0.6 copy-start.5
  48.9 0.6 copy-start.17
  49.0 1.5 %copy-start.3 = (bf16[5,128,128]{1,2,0:T(8,128)(2,1)}, bf16[5,128,128]{1,2,0:T(8,128)(2,1)S(1)}, u32[]{:S(2)}) copy-start(bf16[5,128,128]{1,2,0:T(8,128)(2,1)S(1)} %fusion.23) | copy-start | bytes 491524
  49.2 0.6 copy-start.13
  49.2 0.7 copy-start.15
  49.2 0.7 copy-start.16
  51.2 0.7 copy-start.9
  54.3 74.2 %collective-permute-start.5 = (f32[16,645]{1,0:T(8,128)}, f32[16,645]{1,0:T(8,128)}, u32[]{:S(2)}, u32[]{:S(2)}) collective-permute-start(f32[16,645]{1,0:T(8,128)} %pad_maximum_fusion.2), channel_id=1, source_target_pairs={{0,12},{4,0},{8,4},{12,8},{16,28},{20,16},{24,20},{28,24},{32,44},... | collective-permute-start | bytes 123848 | tf_op jit(solution)/shard_map/ppermute | solution.py:21
  59.6 68.9 %collective-permute-start.4 = (f32[16,645]{1,0:T(8,128)}, f32[16,645]{1,0:T(8,128)}, u32[]{:S(2)}, u32[]{:S(2)}) collective-permute-start(f32[16,645]{1,0:T(8,128)} %pad_maximum_fusion.2), channel_id=1, source_target_pairs={{0,8},{4,12},{8,0},{12,4},{16,24},{20,28},{24,16},{28,20},{32,40},... | collective-permute-start | bytes 123848 | tf_op jit(solution)/shard_map/ppermute | solution.py:21
  61.5 67.0 %collective-permute-start.3 = (f32[16,645]{1,0:T(8,128)}, f32[16,645]{1,0:T(8,128)}, u32[]{:S(2)}, u32[]{:S(2)}) collective-permute-start(f32[16,645]{1,0:T(8,128)} %pad_maximum_fusion.2), channel_id=1, source_target_pairs={{0,4},{4,8},{8,12},{12,0},{16,20},{20,24},{24,28},{28,16},{32,36},... | collective-permute-start | bytes 123848 | tf_op jit(solution)/shard_map/ppermute | solution.py:21
  64.1 0.7 copy-start.11
  107.7 0.9 copy-start.4
  130.2 1.0 copy-start.7
